TPU v7x, 512 devices: a whole 4x4x16 slice. The times are simulated.
512 devices in a mesh: blk: 128 (over z_lo, y, x), off: 4 (over z_hi, core).
Axes of the slice: x: 4, y: 4, z: 16 (z_hi: 2, z_lo: 8; z = z_hi * 8 + z_lo), core: 2. Of those that a mesh axis runs over, the one named last changes fastest.
Arguments:
- coefficients: bfloat16 [2048, 32, 128], P('blk', 'off'), may hold values from -12 to 12
Outputs:
- smoothed: float32 [2048, 32, 128], P(('blk', 'off'))
- log_degree: float32 [2048], P(('blk', 'off'))
All inputs are finite; a program needn't handle non-finite values.
Results may differ from a plain program's by a relative error of at most 0.005.
Values may be sent and summed in bfloat16 or wider, within the bound.
A program may use at most 64 MiB of HBM per device.

v0:
```python
import math

import jax
import jax.numpy as jnp
from jax import lax
from jax.sharding import PartitionSpec as P

epsilon = 1e-06
concentration = 40.0


def shifted(array, axis, by):
    count = lax.axis_size(axis)
    return lax.ppermute(array, axis, [(i, (i + by) % count) for i in range(count)])


def angle_tables(angular):
    half_width = angular // 2
    frequency = jnp.arange(half_width, dtype=jnp.int32)
    shifts = jnp.arange(angular, dtype=jnp.int32)
    product = frequency[:, None] * shifts[None, :] % angular
    phase = product.astype(jnp.float32) * (2.0 * math.pi / angular)
    forward = jnp.concatenate([jnp.cos(phase), -jnp.sin(phase)], axis=0)
    return (forward, forward.T)


def inverse_norms(block_values):
    values = block_values.astype(jnp.float32)
    return lax.rsqrt(jnp.sum(values * values, axis=(1, 2)) + epsilon)


def tile_terms(own_block, own_inverse, other_block, offset, forward, backward):
    row_count = own_block.shape[0]
    half_width = own_block.shape[2] // 2
    highest = lax.Precision.HIGHEST
    other_inverse = inverse_norms(other_block)
    swapped = jnp.concatenate(
        [other_block[:, :, half_width:], other_block[:, :, :half_width]], axis=2
    )
    direct = jnp.einsum("irc,jrc->ijc", own_block, other_block, preferred_element_type=jnp.float32)
    mixed_terms = jnp.einsum("irc,jrc->ijc", own_block, swapped, preferred_element_type=jnp.float32)
    real_part = direct[:, :, :half_width] + direct[:, :, half_width:]
    imag_part = mixed_terms[:, :, half_width:] - mixed_terms[:, :, :half_width]
    cross_spectrum = jnp.concatenate([real_part, imag_part], axis=2).reshape(
        row_count * row_count, -1
    )
    correlation = jnp.dot(
        cross_spectrum, forward, precision=highest, preferred_element_type=jnp.float32
    )
    correlation = correlation.reshape(row_count, row_count, -1)
    cosine = correlation * own_inverse[:, None, None] * other_inverse[None, :, None]
    same_image = jnp.arange(row_count)[:, None] == jnp.arange(row_count)[None, :]
    keep_mask = jnp.where(jnp.logical_and(offset == 0, same_image), 0.0, 1.0).astype(jnp.float32)
    weights = jnp.exp(concentration * cosine) * keep_mask[:, :, None]
    spectral = jnp.dot(
        weights.reshape(row_count * row_count, -1),
        backward,
        precision=highest,
        preferred_element_type=jnp.float32,
    ).reshape(row_count, row_count, -1)
    degree = jnp.sum(spectral[:, :, 0], axis=1)
    rounded = spectral.astype(jnp.bfloat16)
    weight_real = jnp.concatenate([rounded[:, :, :half_width], rounded[:, :, :half_width]], axis=2)
    weight_imag = jnp.concatenate([-rounded[:, :, half_width:], rounded[:, :, half_width:]], axis=2)
    filtered = jnp.einsum(
        "ijc,jrc->irc", weight_real, other_block, preferred_element_type=jnp.float32
    )
    filtered = filtered + jnp.einsum(
        "ijc,jrc->irc", weight_imag, swapped, preferred_element_type=jnp.float32
    )
    return (filtered, degree)


def body(coefficients):
    own_block = lax.all_gather(coefficients, "off", axis=1, tiled=True)
    own_inverse = inverse_norms(own_block)
    row_count, radial, angular = own_block.shape
    forward, backward = angle_tables(angular)
    ranges = lax.axis_size("off")
    per_range = min(8, lax.axis_size("blk") // ranges)
    range_index = lax.axis_index("off")
    range_base = range_index * per_range
    packet = own_block
    for bit_number in range(ranges.bit_length() - 1):
        moved_packet = shifted(packet, "blk", -(per_range << bit_number))
        chosen = range_index // (1 << bit_number) % 2 == 1
        packet = jnp.where(chosen, moved_packet, packet)
    empty_sum = jnp.zeros((row_count, radial, angular), jnp.float32)
    empty_degree = jnp.zeros((row_count,), jnp.float32)

    def advance_one(step, loop_state):
        filtered, degree, current = loop_state
        terms = tile_terms(own_block, own_inverse, current, range_base + step, forward, backward)
        current = shifted(current, "blk", -1)
        return (filtered + terms[0], degree + terms[1], current)

    last_step = per_range - 1
    filtered, degree, current = lax.fori_loop(
        0, last_step, advance_one, (empty_sum, empty_degree, packet)
    )
    terms = tile_terms(own_block, own_inverse, current, range_base + last_step, forward, backward)
    filtered = filtered + terms[0]
    degree = degree + terms[1]
    totals = (
        lax.psum_scatter(filtered, "off", scatter_dimension=0, tiled=True),
        lax.psum_scatter(degree, "off", scatter_dimension=0, tiled=True),
    )
    smoothed = totals[0] / totals[1][:, None, None]
    return (smoothed, jnp.log(totals[1]))


def solution(mesh):
    return jax.shard_map(
        body,
        mesh=mesh,
        in_specs=(P("blk", "off", None),),
        out_specs=(P(("blk", "off"), None, None), P(("blk", "off"))),
        check_vma=False,
    )
```

profile of v0, /device:TPU:25, one launch (start us, length us, event | category | flops | bytes accessed | tf_op | source)
XLA Modules:
  0.0 277.5 jit_solution(10738338174467296353)
XLA Ops:
  8.2 27.8 %all_gather.3 = bf16[16,32,128]{0,1,2:T(8,128)(2,1)S(1)} all-gather(bf16[16,8,128]{0,1,2:T(8,128)(2,1)S(1)} %copy.20), channel_id=1, replica_groups=mesh['blk'=128,'off'=4] {'off'}, dimensions={1}, use_global_device_ids=true | all-gather | bytes 163840 | tf_op jit(solution)/shard_map/all_gather | solution.py:75
  36.1 1.2 copy.21
  37.2 2.9 %collective-permute-start.1 = (bf16[16,32,128]{2,1,0:T(8,128)(2,1)S(1)}, bf16[16,32,128]{2,1,0:T(8,128)(2,1)S(1)}, u32[]{:S(2)}, u32[]{:S(2)}) collective-permute-start(bf16[16,32,128]{2,1,0:T(8,128)(2,1)S(1)} %copy.21), channel_id=1, source_target_pairs={{0,480},{4,484},{8,488},{12,492},{16,496},{20,500},{24,504},{28,50... | collective-permute-start | bytes 393224 | tf_op jit(solution)/shard_map/ppermute | solution.py:14
  40.9 15.4 %collective-permute-done.1 = bf16[16,32,128]{2,1,0:T(8,128)(2,1)S(1)} collective-permute-done((bf16[16,32,128]{2,1,0:T(8,128)(2,1)S(1)}, bf16[16,32,128]{2,1,0:T(8,128)(2,1)S(1)}, u32[]{:S(2)}, u32[]{:S(2)}) %collective-permute-start.1) | collective-permute-done | bytes 131104 | tf_op jit(solution)/shard_map/ppermute | solution.py:14
  56.3 2.4 copy.22
  58.7 1.3 broadcast_select_fusion.1
  60.0 1.2 copy.23
  61.2 8.7 %collective-permute-start.2 = (bf16[16,32,128]{2,1,0:T(8,128)(2,1)S(1)}, bf16[16,32,128]{2,1,0:T(8,128)(2,1)S(1)}, u32[]{:S(2)}, u32[]{:S(2)}) collective-permute-start(bf16[16,32,128]{2,1,0:T(8,128)(2,1)S(1)} %copy.23), channel_id=1, source_target_pairs={{0,448},{4,452},{8,456},{12,460},{16,464},{20,468},{24,472},{28,47... | collective-permute-start | bytes 393224 | tf_op jit(solution)/shard_map/ppermute | solution.py:14
  71.1 1.8 collective-permute-done.2
  72.9 1.5 copy.24
  75.5 2.5 copy.25
  78.0 82.3 %while.18 = (s32[]{:T(128)}, f32[16,32,128]{1,0,2:T(8,128)}, f32[16]{0:T(128)}, bf16[16,32,128]{2,1,0:T(8,128)(2,1)S(1)}, bf16[16,32,128]{1,0,2:T(8,128)(2,1)S(1...) while((s32[]{:T(128)}, f32[16,32,128]{1,0,2:T(8,128)}, ...), condition=%wide.region_4.5_spmd.clone, body=%wide.region_1.4_spmd.clone.sunk | while | flops 110216208 | bytes 6230326 | solution.py:98
  78.2 4.6 %collective-permute-start = (bf16[16,32,128]{2,1,0:T(8,128)(2,1)S(1)}, bf16[16,32,128]{2,1,0:T(8,128)(2,1)S(1)}, u32[]{:S(2)}, u32[]{:S(2)}) collective-permute-start(bf16[16,32,128]{2,1,0:T(8,128)(2,1)S(1)} %copy.56), channel_id=1, source_target_pairs={{0,508},{4,0},{8,4},{12,8},{16,12},{20,16},{24,20},{28,24},{32,28}... | collective-permute-start | bytes 393224 | tf_op jit(solution)/shard_map/while/body/eval_jaxpr/ppermute | solution.py:14
  88.8 1.5 fusion.95
  90.8 2.5 collective-permute-start
  99.2 2.7 fusion.95
  102.5 2.2 collective-permute-start
  110.6 2.7 fusion.95
  113.9 2.2 collective-permute-start
  122.1 2.7 fusion.95
  125.4 2.6 collective-permute-start
  133.9 2.7 fusion.95
  137.2 2.4 collective-permute-start
  145.6 2.7 fusion.95
  148.9 2.2 collective-permute-start
  157.1 2.7 fusion.95
  165.0 1.4 fusion.44
  166.9 1.6 fusion.17
  169.7 1.3 dynamic-slice
  171.8 16.4 %all-reduce = f32[16]{0:T(128)S(1)} all-reduce(f32[16]{0:T(128)S(1)} %add.125), channel_id=3, replica_groups=mesh['blk'=128,'off'=4] {'off'}, use_global_device_ids=true, to_apply=%region_8.9.clone | all-reduce | flops 16 | bytes 128
  188.8 80.3 %reduce-scatter.2.cloned.1.call-done = f32[4,32,128]{2,1,0:T(8,128)} async-done(((f32[16,32,128]{2,1,0:T(8,128)}), f32[4,32,128]{2,1,0:T(8,128)}) %reduce-scatter.2.cloned.1.call-update) | async-done | bytes 65552 | tf_op jit(solution)/shard_map/reduce_scatter | solution.py:105
  269.1 1.5 broadcast_divide_fusion
  (248 shorter events, 55.9 us)
Async XLA Ops:
  7.2 261.9 %reduce-scatter.2.cloned.1.call-start = ((), (), s32[]{:S(2)}) async-start(), calls=%async_computation.1 | async-start | bytes 327680 | tf_op jit(solution)/shard_map/reduce_scatter | solution.py:105
  36.1 33.9 %copy-start = (bf16[16,32,128]{0,1,2:T(8,128)(2,1)}, bf16[16,32,128]{0,1,2:T(8,128)(2,1)S(1)}, u32[]{:S(2)}) copy-start(bf16[16,32,128]{0,1,2:T(8,128)(2,1)S(1)} %all_gather.3) | copy-start | bytes 393220
  37.2 19.0 %collective-permute-start.1 = (bf16[16,32,128]{2,1,0:T(8,128)(2,1)S(1)}, bf16[16,32,128]{2,1,0:T(8,128)(2,1)S(1)}, u32[]{:S(2)}, u32[]{:S(2)}) collective-permute-start(bf16[16,32,128]{2,1,0:T(8,128)(2,1)S(1)} %copy.21), channel_id=1, source_target_pairs={{0,480},{4,484},{8,488},{12,492},{16,496},{20,500},{24,504},{28,50... | collective-permute-start | bytes 393224 | tf_op jit(solution)/shard_map/ppermute | solution.py:14
  40.8 29.0 %copy-start.3 = (f32[64,128]{1,0:T(8,128)}, f32[64,128]{1,0:T(8,128)S(1)}, u32[]{:S(2)}) copy-start(f32[64,128]{1,0:T(8,128)S(1)} %get-tuple-element.249) | copy-start | bytes 98308
  40.9 29.0 %copy-start.5 = (f32[64,128]{1,0:T(8,128)}, f32[64,128]{1,0:T(8,128)S(1)}, u32[]{:S(2)}) copy-start(f32[64,128]{1,0:T(8,128)S(1)} %get-tuple-element.250) | copy-start | bytes 98308
  61.2 11.7 %collective-permute-start.2 = (bf16[16,32,128]{2,1,0:T(8,128)(2,1)S(1)}, bf16[16,32,128]{2,1,0:T(8,128)(2,1)S(1)}, u32[]{:S(2)}, u32[]{:S(2)}) collective-permute-start(bf16[16,32,128]{2,1,0:T(8,128)(2,1)S(1)} %copy.23), channel_id=1, source_target_pairs={{0,448},{4,452},{8,456},{12,460},{16,464},{20,468},{24,472},{28,47... | collective-permute-start | bytes 393224 | tf_op jit(solution)/shard_map/ppermute | solution.py:14
  78.2 12.0 %collective-permute-start = (bf16[16,32,128]{2,1,0:T(8,128)(2,1)S(1)}, bf16[16,32,128]{2,1,0:T(8,128)(2,1)S(1)}, u32[]{:S(2)}, u32[]{:S(2)}) collective-permute-start(bf16[16,32,128]{2,1,0:T(8,128)(2,1)S(1)} %copy.56), channel_id=1, source_target_pairs={{0,508},{4,0},{8,4},{12,8},{16,12},{20,16},{24,20},{28,24},{32,28}... | collective-permute-start | bytes 393224 | tf_op jit(solution)/shard_map/while/body/eval_jaxpr/ppermute | solution.py:14
  88.7 1.5 copy-start.7
  90.2 0.6 copy-start.8
  90.8 11.1 %collective-permute-start = (bf16[16,32,128]{2,1,0:T(8,128)(2,1)S(1)}, bf16[16,32,128]{2,1,0:T(8,128)(2,1)S(1)}, u32[]{:S(2)}, u32[]{:S(2)}) collective-permute-start(bf16[16,32,128]{2,1,0:T(8,128)(2,1)S(1)} %copy.56), channel_id=1, source_target_pairs={{0,508},{4,0},{8,4},{12,8},{16,12},{20,16},{24,20},{28,24},{32,28}... | collective-permute-start | bytes 393224 | tf_op jit(solution)/shard_map/while/body/eval_jaxpr/ppermute | solution.py:14
  99.2 2.7 copy-start.7
  101.9 0.6 copy-start.8
  102.5 10.8 %collective-permute-start = (bf16[16,32,128]{2,1,0:T(8,128)(2,1)S(1)}, bf16[16,32,128]{2,1,0:T(8,128)(2,1)S(1)}, u32[]{:S(2)}, u32[]{:S(2)}) collective-permute-start(bf16[16,32,128]{2,1,0:T(8,128)(2,1)S(1)} %copy.56), channel_id=1, source_target_pairs={{0,508},{4,0},{8,4},{12,8},{16,12},{20,16},{24,20},{28,24},{32,28}... | collective-permute-start | bytes 393224 | tf_op jit(solution)/shard_map/while/body/eval_jaxpr/ppermute | solution.py:14
  110.6 2.7 copy-start.7
  113.3 0.6 copy-start.8
  113.9 10.8 %collective-permute-start = (bf16[16,32,128]{2,1,0:T(8,128)(2,1)S(1)}, bf16[16,32,128]{2,1,0:T(8,128)(2,1)S(1)}, u32[]{:S(2)}, u32[]{:S(2)}) collective-permute-start(bf16[16,32,128]{2,1,0:T(8,128)(2,1)S(1)} %copy.56), channel_id=1, source_target_pairs={{0,508},{4,0},{8,4},{12,8},{16,12},{20,16},{24,20},{28,24},{32,28}... | collective-permute-start | bytes 393224 | tf_op jit(solution)/shard_map/while/body/eval_jaxpr/ppermute | solution.py:14
  122.1 2.7 copy-start.7
  124.8 0.6 copy-start.8
  125.4 11.3 %collective-permute-start = (bf16[16,32,128]{2,1,0:T(8,128)(2,1)S(1)}, bf16[16,32,128]{2,1,0:T(8,128)(2,1)S(1)}, u32[]{:S(2)}, u32[]{:S(2)}) collective-permute-start(bf16[16,32,128]{2,1,0:T(8,128)(2,1)S(1)} %copy.56), channel_id=1, source_target_pairs={{0,508},{4,0},{8,4},{12,8},{16,12},{20,16},{24,20},{28,24},{32,28}... | collective-permute-start | bytes 393224 | tf_op jit(solution)/shard_map/while/body/eval_jaxpr/ppermute | solution.py:14
  133.9 2.7 copy-start.7
  136.6 0.6 copy-start.8
  137.2 11.1 %collective-permute-start = (bf16[16,32,128]{2,1,0:T(8,128)(2,1)S(1)}, bf16[16,32,128]{2,1,0:T(8,128)(2,1)S(1)}, u32[]{:S(2)}, u32[]{:S(2)}) collective-permute-start(bf16[16,32,128]{2,1,0:T(8,128)(2,1)S(1)} %copy.56), channel_id=1, source_target_pairs={{0,508},{4,0},{8,4},{12,8},{16,12},{20,16},{24,20},{28,24},{32,28}... | collective-permute-start | bytes 393224 | tf_op jit(solution)/shard_map/while/body/eval_jaxpr/ppermute | solution.py:14
  145.6 2.7 copy-start.7
  148.3 0.6 copy-start.8
  148.9 10.8 %collective-permute-start = (bf16[16,32,128]{2,1,0:T(8,128)(2,1)S(1)}, bf16[16,32,128]{2,1,0:T(8,128)(2,1)S(1)}, u32[]{:S(2)}, u32[]{:S(2)}) collective-permute-start(bf16[16,32,128]{2,1,0:T(8,128)(2,1)S(1)} %copy.56), channel_id=1, source_target_pairs={{0,508},{4,0},{8,4},{12,8},{16,12},{20,16},{24,20},{28,24},{32,28}... | collective-permute-start | bytes 393224 | tf_op jit(solution)/shard_map/while/body/eval_jaxpr/ppermute | solution.py:14
  157.0 2.7 copy-start.7
  159.8 0.6 copy-start.8
  160.5 1.2 copy-start.1
  162.9 0.8 copy-start.4
  163.0 0.8 copy-start.6
  165.0 1.9 copy-start.2
  168.5 3.3 %copy-start.9 = (f32[16]{0:T(128)S(1)}, f32[16]{0:T(128)}, u32[]{:S(2)}) copy-start(f32[16]{0:T(128)} %get-tuple-element.160) | copy-start | bytes 196
Sparse Core Ops, SparseCore 0:
  169.8 99.2 reduce-scatter.1
where the time goes:
time: 280 us; the launch traced here: 277 us
  waiting for transfers between devices  97.5 us (35%)
  blocking collectives  44.2 us (16%)
  matrix products  40.1 us (14%)
  local copies, waits for them, and re-layouts  37.3 us (13%)
  starting transfers between devices  30.2 us (11%)
  between operations  15 us (5%)
  other arithmetic  11.9 us (4%)
    reduce_scatter x1, waiting for transfers between devices, body(): lax.psum_scatter(filtered, 'off', scatter_dimension=0, tiled=True)  80.3 us
    ppermute x9, starting transfers between devices, shifted(): lax.ppermute(array, axis, [(i, (i + by) % count) for i in range(count)])  30.1 us
    all_gather x1, blocking collectives, body(): own_block = lax.all_gather(coefficients, 'off', axis=1, tiled=True)  27.8 us
    dot_general x8, matrix products, tile_terms(): jnp.einsum('ijc,jrc->irc', weight_imag, swapped, preferred_element_type=j...  19.2 us
    ppermute x9, waiting for transfers between devices, shifted(): lax.ppermute(array, axis, [(i, (i + by) % count) for i in range(count)])  17.2 us
    unnamed x1, blocking collectives  16.4 us
    dot_general x8, matrix products, tile_terms(): jnp.dot(weights.reshape(row_count * row_count, -1), backward, precision=h...  7.99 us
    while x42, local copies, waits for them, and re-layouts  7.01 us
  transfers between devices with their start and end apart: 10, of which 3 were waited for; matrix products, arithmetic and copies ran while one was open for 22% of the time, Pallas kernels for 0%

commit v1 on v0

v1 whole, which is shorter than its diff:
```python
import functools
import math

import jax
import jax.numpy as jnp
from jax import lax
from jax.experimental import pallas as pl
from jax.experimental.pallas import tpu as pltpu
from jax.sharding import PartitionSpec as P

MESH = pl.DeviceIdType.MESH
epsilon = 1e-06
concentration = 40.0
f32, bf16 = jnp.float32, jnp.bfloat16


def nt(a, b):
    return lax.dot_general(a, b, (((1,), (1,)), ((), ())), preferred_element_type=f32)


def nn(a, b):
    return jnp.dot(a, b, preferred_element_type=f32)


def split(a):
    high = a.astype(bf16)
    return high, (a - high.astype(f32)).astype(bf16)


def iota(shape, dim):
    return lax.broadcasted_iota(jnp.int32, shape, dim)


def lane_bit(shape, bit):
    return iota(shape, len(shape) - 1) // bit % 2 == 1


def lane_roll(a, by):
    return pltpu.roll(a, by % 128, a.ndim - 1)


def rotate_parts(a, sign):
    imag = lane_bit(a.shape, 8)
    return jnp.where(imag, -sign * lane_roll(a, 8), sign * lane_roll(a, -8))


def body_kernel(
    x_ref, out_ref, log_ref,
    own, yf, o_buf, g_buf, l_buf, xb, lhs, s_buf, spec, acc, fb, rb,
    ss_z, rs_z, ss_l, rs_l, ss_o, rs_o, ss_a, rs_a, ss_x, rs_x, ss_f, rs_f,
):
    b, o = lax.axis_index("blk"), lax.axis_index("off")
    x, y, z_lo = b % 4, b // 4 % 4, b // 16
    z_hi, c = o // 2, o % 2
    z = z_hi * 8 + z_lo
    along, across = x * (1 - c) + y * c, y * (1 - c) + x * c

    def device(dx, dy, dz, core):
        zz = (z + dz) % 16
        return (zz % 8 * 16 + (y + dy) % 4 * 4 + (x + dx) % 4, zz // 8 * 2 + core)

    def along_peer(d):
        return device(d * (1 - c), d * c, 0, c)

    def across_peer(d, core):
        return device(d * c, d * (1 - c), 0, core)

    def remote(src, dst, send, recv, to):
        return pltpu.make_async_remote_copy(
            src_ref=src, dst_ref=dst, send_sem=send, recv_sem=recv,
            device_id=to, device_id_type=MESH,
        )

    partner = device(0, 0, 0, 1 - c)
    barrier = pltpu.get_barrier_semaphore()
    peers = [partner] + [device(0, 0, d, c) for d in (-2, -1, 1, 2)]
    for d in (1, 2, 3):
        for core in (0, 1):
            peers += [device(d, 0, 0, core), device(0, d, 0, core)]
    for peer in peers:
        pl.semaphore_signal(barrier, inc=1, device_id=peer, device_id_type=MESH)

    place = iota((128, 128), 1)
    source = place // 8 % 2 * 64 + place // 16 * 8 + place % 8
    permute = jnp.where(iota((128, 128), 0) == source, 1.0, 0.0).astype(bf16)
    yf[...] = nn(x_ref[...].astype(f32).reshape(128, 128).astype(bf16), permute)
    rows = [yf[pl.ds(r, 16, stride=8), :] for r in range(8)]
    for bit in (1, 2, 4):
        upper = lane_bit((16, 128), 16 * bit)
        for r in range(8):
            if r & bit == 0:
                low, high = rows[r], rows[r | bit]
                rows[r] = jnp.where(upper, lane_roll(high, 16 * bit), low)
                rows[r | bit] = jnp.where(upper, high, lane_roll(low, -16 * bit))
    for k in range(8):
        tile = rows[k].astype(bf16)
        own[k] = tile
        g_buf[0, 0, k, along] = tile
        o_buf[0, c, k] = tile

    pl.semaphore_wait(barrier, len(peers))

    sends = []

    def go(copy):
        copy.start()
        sends.append(copy)
        return copy

    def z_copy(src, h, plane, dz):
        return remote(src, g_buf.at[h, plane, :, along], ss_z.at[h, plane], rs_z.at[h, plane], device(0, 0, dz, c))

    def l_copy(src, n):
        return remote(src, l_buf.at[n], ss_l.at[n], rs_l.at[n], device(0, 0, 2, c))

    def o_copy(src, h, path):
        return remote(src, o_buf.at[h, path], ss_o.at[h], rs_o.at[h], partner)

    def a_copy(h, plane, d, place):
        return remote(
            g_buf.at[h, plane, :, place], g_buf.at[h, plane, :, place],
            ss_a.at[h, plane, d - 1], rs_a.at[h, plane, d - 1], along_peer(d),
        )

    def send_along(h, plane):
        for d in (1, 2, 3):
            go(a_copy(h, plane, d, along))

    def wait_along(h):
        for plane in (2, 1, 0):
            for d in (1, 2, 3):
                a_copy(h, plane, d, (along + 4 - d) % 4).wait_recv()

    def plane_of(a, d):
        mine = (4 * across + a) * (1 - c) + (4 * a + across) * c
        theirs_across = (across + d) % 4
        theirs = (4 * theirs_across + along) * (1 - c) + (4 * along + theirs_across) * c
        return (theirs - mine + 15) // 16 * 2

    def half_of(h, plane):
        return (h + (z_lo + plane) // 8) % 2

    def send_across(h):
        def to_first(d):
            return remote(
                g_buf.at[h, 1], xb.at[half_of(h, 1), c, :, across],
                ss_x.at[h, d], rs_x.at[h, c, d], across_peer(d, 0),
            )

        def to_second(d, a):
            plane = plane_of(a, d)
            return remote(
                g_buf.at[h, plane, :, a], xb.at[half_of(h, plane), c, :, across, a],
                ss_x.at[h, d], rs_x.at[h, c, d], across_peer(d, 1),
            )

        for d in (1, 3, 2):
            to_first(d).start()
            for a in range(4):
                to_second(d, a).start()

        @pl.when(c == 0)
        def _():
            for a in range(4):
                to_second(0, a).start()
            pltpu.make_async_copy(
                g_buf.at[h, 1], xb.at[half_of(h, 1), c, :, across], rs_x.at[h, c, 0]
            ).start()

        @pl.when(c == 1)
        def _():
            to_first(0).start()
            for a in range(4):
                plane = plane_of(a, 0)
                pltpu.make_async_copy(
                    g_buf.at[h, plane, :, a], xb.at[half_of(h, plane), c, :, across, a], rs_x.at[h, c, 0]
                ).start()

    def wait_across(h):
        for path, mid in ((0, y), (1, x)):
            for d in range(4):
                place = (mid + 4 - d) % 4
                region = xb.at[h, path, :, place]
                pltpu.make_async_copy(region, region, rs_x.at[h, path, d]).wait()

    go(l_copy(own, 0))
    go(z_copy(own, 0, 2, -2))
    go(z_copy(own, 0, 1, -1))
    go(o_copy(own, 0, c))
    send_along(0, 0)

    def frequency_of(q):
        k, u = q // 16, q % 8
        return 8 * k + (k - u + 8) % 8, q // 8 % 2

    def table(q_dim):
        q, s = iota((128, 128), q_dim), iota((128, 128), 1 - q_dim)
        m, part = frequency_of(q)
        phase = (m * s % 128).astype(f32) * (2.0 * math.pi / 128)
        return jnp.where(part == 0, jnp.cos(phase), -jnp.sin(phase))

    f_high, f_low = split(table(1))
    forward = jnp.concatenate([f_high, f_high, f_low], axis=1)
    b_high, b_low = split(table(0))
    backward = jnp.concatenate([b_high, b_high, b_low], axis=1)

    def matches(k):
        u, t = iota((8, 128), 0), iota((8, 128), 1) % 8
        return (u + t) % 8 == k

    def build_lhs(h):
        squares = jnp.zeros((8, 128), f32)
        for path in (0, 1):
            for k in range(8):
                both = o_buf[h, path, k].astype(f32)
                rows = jnp.where(z_hi == 0, both[:8], both[8:])
                squares = squares + rows * rows
                turned = rotate_parts(rows, 1.0)
                pair = [jnp.where(matches(k)[None], v[:, None, :], 0.0) for v in (rows, turned)]
                block = jnp.concatenate(pair, axis=1).reshape(128, 128)
                lhs[h, k, :, path * 128 : path * 128 + 128] = block.astype(bf16)
        return squares

    def tile_of(h, path, k):
        if path == 0:
            return xb[h, 0, k].reshape(256, 128)
        return jnp.concatenate([xb[h, 1, k, a, bb] for bb in range(4) for a in range(4)], axis=0)

    def cross(squares):
        for k in range(8):
            tiles = [tile_of(h, path, k) for h in (0, 1) for path in (0, 1)]
            for t in tiles:
                wide = t.astype(f32)
                squares = squares + wide * wide
            left = jnp.concatenate([lhs[0, k], lhs[1, k]], axis=1)
            s_buf[k] = nt(left, jnp.concatenate(tiles, axis=1))
        return squares

    l_copy(own, 0).wait_recv()
    go(l_copy(l_buf.at[0], 1))
    z_copy(own, 0, 1, -1).wait_recv()
    send_along(0, 1)
    z_copy(own, 0, 2, -2).wait_recv()
    send_along(0, 2)
    l_copy(own, 1).wait_recv()
    go(z_copy(l_buf.at[1], 1, 2, 2))
    wait_along(0)
    send_across(0)
    z_copy(own, 1, 2, 2).wait_recv()
    go(z_copy(g_buf.at[1, 2, :, along], 1, 0, 2))
    go(z_copy(g_buf.at[1, 2, :, along], 1, 1, 1))
    send_along(1, 2)
    o_copy(own, 0, 1 - c).wait_recv()
    own_squares = build_lhs(0)
    z_copy(own, 1, 1, 1).wait_recv()
    send_along(1, 1)
    z_copy(own, 1, 0, 2).wait_recv()
    send_along(1, 0)
    go(o_copy(g_buf.at[1, 0, :, along], 1, c))
    for k in range(8):
        o_buf[1, c, k] = g_buf[1, 0, k, along]
    wait_across(0)
    wait_along(1)
    send_across(1)
    o_copy(own, 1, 1 - c).wait_recv()
    own_squares = own_squares + build_lhs(1)
    wait_across(1)
    squares = cross(jnp.zeros((256, 128), f32))

    def pieces(a):
        high, low = split(a)
        rest = (a - high.astype(f32) - low.astype(f32)).astype(bf16)
        return [high, low, rest]

    ones = jnp.ones((8, 384), bf16)
    norm_squares = nt(ones, jnp.concatenate(pieces(squares), axis=1))
    own_norm = jnp.sum(own_squares, axis=1, keepdims=True)
    gain = lax.rsqrt(norm_squares + epsilon) * (concentration * lax.rsqrt(own_norm + epsilon))

    lane = iota((128, 256), 1)
    own_lane = jnp.where(c == 1, (y * 4 + x) * 16 + z_hi * 8, -1000)
    for i in range(8):
        s_i = jnp.concatenate([s_buf[k, i * 16 : i * 16 + 16, :] for k in range(8)], axis=0)
        high, low = split(s_i)
        correlation = nn(forward, jnp.concatenate([high, low, high], axis=0))
        weights = jnp.exp(correlation * gain[i : i + 1])
        weights = jnp.where(lane == own_lane + i, 0.0, weights)
        high, low = split(weights)
        spectral = nn(backward, jnp.concatenate([high, low, high], axis=0))
        degree = jnp.sum(spectral[0:1], axis=1, keepdims=True)
        fb[i, 4] = jnp.broadcast_to(degree, (8, 128))
        rounded = spectral.astype(bf16)
        for k in range(8):
            spec[k, i * 16 : i * 16 + 16, :] = rounded[k * 16 : k * 16 + 16]

    for k in range(8):
        keep = jnp.concatenate([matches(k)] * 16, axis=0)
        for h in (0, 1):
            for path in (0, 1):
                part = nn(spec[k], tile_of(h, path, k))
                n = 2 * h + path
                acc[n] = part if k == 0 else jnp.where(keep, part, acc[n])
    for n in range(4):
        pair = acc[n].reshape(8, 16, 128)
        total = pair[:, :8] + rotate_parts(pair[:, 8:], -1.0)
        for i in range(8):
            fb[i, n] = total[i]

    last = remote(fb.at[pl.ds((1 - c) * 4, 4)], rb, ss_f, rs_f, partner)
    last.start()
    last.wait()
    total = fb[pl.ds(c * 4, 4)] + rb[...]
    degree = total[:, 4:5]
    v = (total[:, :4] / degree).reshape(16, 8, 128)
    for bit in (1, 2, 4):
        v = jnp.where(lane_bit(v.shape, bit), pltpu.roll(v, bit, 1), v)
    for bit in (1, 2, 4):
        group = lane_bit(v.shape, 16 * bit)
        row = iota(v.shape, 1) // bit % 2 == 1
        down = lane_roll(pltpu.roll(v, 8 - bit, 1), 16 * bit)
        up = lane_roll(pltpu.roll(v, bit, 1), -16 * bit)
        v = jnp.where(group == row, v, jnp.where(group, down, up))
    flat = sum(nt(p, permute) for p in pieces(v.reshape(128, 128)))
    flat = flat.reshape(4, 4, 8, 128)
    for h in (0, 1):
        for path in (0, 1):
            start = pl.multiple_of(((z_hi + h) % 2 * 2 + path) * 8, 8)
            out_ref[:, pl.ds(start, 8), :] = flat[:, 2 * h + path]
    logs = jnp.log(degree[:, 0])
    pick = iota((8, 128), 1)
    line = jnp.zeros((8, 128), f32)
    for i in range(4):
        line = jnp.where(pick == i, logs[i], line)
    log_ref[...] = line

    for copy in sends:
        copy.wait_send()
    for h in (0, 1):
        for d in (1, 2, 3):
            both = g_buf.at[h, pl.ds(0, 2)]
            remote(both, both, ss_x.at[h, d], rs_x.at[h, 0, d], partner).wait_send()
        one = g_buf.at[h, 0]
        remote(one, one, ss_x.at[h, 0], rs_x.at[h, 0, 0], partner).wait_send()


def body(coefficients):
    vmem = pl.BlockSpec(memory_space=pltpu.VMEM)
    dma = pltpu.SemaphoreType.DMA
    smoothed, logs = pl.pallas_call(
        body_kernel,
        out_shape=(
            jax.ShapeDtypeStruct((4, 32, 128), f32),
            jax.ShapeDtypeStruct((8, 128), f32),
        ),
        in_specs=[vmem],
        out_specs=(vmem, vmem),
        scratch_shapes=[
            pltpu.VMEM((8, 16, 128), bf16),
            pltpu.VMEM((128, 128), f32),
            pltpu.VMEM((2, 2, 8, 16, 128), bf16),
            pltpu.VMEM((2, 3, 8, 4, 16, 128), bf16),
            pltpu.VMEM((2, 8, 16, 128), bf16),
            pltpu.VMEM((2, 2, 8, 4, 4, 16, 128), bf16),
            pltpu.VMEM((2, 8, 128, 256), bf16),
            pltpu.VMEM((8, 128, 256), f32),
            pltpu.VMEM((8, 128, 256), bf16),
            pltpu.VMEM((4, 128, 128), f32),
            pltpu.VMEM((8, 5, 8, 128), f32),
            pltpu.VMEM((4, 5, 8, 128), f32),
            dma((2, 3)), dma((2, 3)),
            dma((2,)), dma((2,)),
            dma((2,)), dma((2,)),
            dma((2, 3, 3)), dma((2, 3, 3)),
            dma((2, 4)), dma((2, 2, 4)),
            dma, dma,
        ],
        compiler_params=pltpu.CompilerParams(collective_id=0, has_side_effects=True),
        name="graph_filter",
    )(coefficients)
    return smoothed, logs[0, :4]


def solution(mesh):
    return jax.shard_map(
        body,
        mesh=mesh,
        in_specs=(P("blk", "off", None),),
        out_specs=(P(("blk", "off"), None, None), P(("blk", "off"))),
        check_vma=False,
    )
```

time: 280 us -> 52.6 us (0.19)
  waiting for transfers between devices: 97.5 us -> 0 us
  Pallas kernels: 0 us -> 48.4 us
  blocking collectives: 44.2 us -> 0 us
  matrix products: 40.1 us -> 0 us
  local copies, waits for them, and re-layouts: 37.3 us -> 2.66 us
  starting transfers between devices: 30.2 us -> 0 us
  between operations: 15 us -> 0.64 us
  other arithmetic: 11.9 us -> 0 us
    reduce_scatter x1 -> x0, waiting for transfers between devices: 80.3 us -> none  [body(): lax.psum_scatter(filtered, 'off', scatter_dimension=0, tiled=True)]
    pallas_call x0 -> x1, Pallas kernels: none -> 48.4 us  [body(): pl.pallas_call(body_kernel, out_shape=(jax.ShapeDtypeStruct((4, 32, 128),...]
    dot_general x48 -> x0, matrix products: 40.1 us -> none  [the longest x8 19.2 us: tile_terms(): jnp.einsum('ijc,jrc->irc', weight_imag, swapped, preferred_element_type=j...]
    ppermute x9 -> x0, starting transfers between devices: 30.1 us -> none  [shifted(): lax.ppermute(array, axis, [(i, (i + by) % count) for i in range(count)])]
    all_gather x1 -> x0, blocking collectives: 27.8 us -> none  [body(): own_block = lax.all_gather(coefficients, 'off', axis=1, tiled=True)]
    ppermute x9 -> x0, waiting for transfers between devices: 17.2 us -> none  [shifted(): lax.ppermute(array, axis, [(i, (i + by) % count) for i in range(count)])]
    unnamed x1 -> x0, blocking collectives: 16.4 us -> none
    concatenate x24 -> x0, local copies, waits for them, and re-layouts: 10.3 us -> none  [the longest x8 3.44 us: tile_terms(): jnp.concatenate([-rounded[:, :, half_width:], rounded[:, :, half_width:]]...]
  transfers between devices with their start and end apart: 10 -> 0, of which waited for: 3 -> 0; matrix products, arithmetic and copies ran while one was open for 22% -> 0% of each run, Pallas kernels for 0% -> 0%
where the time goes in v1:
time: 52.6 us; the launch traced here: 51.7 us
  Pallas kernels  48.4 us (92%)
  local copies, waits for them, and re-layouts  2.66 us (5%)
  between operations  0.64 us (1%)
    pallas_call x1, Pallas kernels, body(): pl.pallas_call(body_kernel, out_shape=(jax.ShapeDtypeStruct((4, 32, 128),...  48.4 us
    unnamed x1, local copies, waits for them, and re-layouts  1.47 us
    squeeze x1, local copies, waits for them, and re-layouts, body(): return (smoothed, logs[0, :4])  1.19 us

profile of v1, /device:TPU:25, one launch (start us, length us, event | category | flops | bytes accessed | tf_op | source)
XLA Modules:
  0.0 51.7 jit_solution(12067867996621836172)
XLA Ops:
  0.6 48.4 %graph_filter.1 = (f32[4,32,128]{2,1,0:T(8,128)}, f32[8,128]{1,0:T(8,128)}) custom-call(bf16[16,8,128]{2,1,0:T(8,128)(2,1)} %x_ref.1), custom_call_target="tpu_custom_call" | custom-call | tf_op jit(solution)/shard_map/graph_filter/pallas_call | solution.py:349
  49.1 1.2 %slice_bitcast_fusion = f32[4]{0:T(128)} fusion(f32[8,128]{1,0:T(8,128)} %get-tuple-element.5), kind=kLoop, calls=%fused_computation | loop fusion | bytes 32 | tf_op jit(solution)/shard_map/squeeze | solution.py:380
  50.3 1.5 %copy.4 = f32[4,32,128]{2,1,0:T(8,128)} copy(f32[4,32,128]{2,1,0:T(8,128)} %get-tuple-element.8) | data formatting | bytes 131072

commit v2 on v1

v2 whole, which is shorter than its diff:
```python
import functools
import functools
import math

import jax
import jax.numpy as jnp
from jax import lax
from jax.experimental import pallas as pl
from jax.experimental.pallas import tpu as pltpu
from jax.sharding import PartitionSpec as P

MESH = pl.DeviceIdType.MESH
epsilon = 1e-06
concentration = 40.0
f32, bf16 = jnp.float32, jnp.bfloat16


def nt(a, b):
    return lax.dot_general(a, b, (((1,), (1,)), ((), ())), preferred_element_type=f32)


def nn(a, b):
    return jnp.dot(a, b, preferred_element_type=f32)


def split(a):
    high = a.astype(bf16)
    return high, (a - high.astype(f32)).astype(bf16)


def iota(shape, dim):
    return lax.broadcasted_iota(jnp.int32, shape, dim)


def lane_bit(shape, bit):
    return iota(shape, len(shape) - 1) // bit % 2 == 1


def lane_roll(a, by):
    return pltpu.roll(a, by % 128, a.ndim - 1)


def rotate_parts(a, sign):
    imag = lane_bit(a.shape, 8)
    return jnp.where(imag, -sign * lane_roll(a, 8), sign * lane_roll(a, -8))


places = [
    (0, 0), (0, 1), (1, 0), (0, 3), (3, 0), (0, 2), (2, 0), (1, 1),
    (1, 3), (3, 1), (3, 3), (1, 2), (2, 1), (3, 2), (2, 3), (2, 2),
]
slot_of = {place: n for n, place in enumerate(places)}


def body_kernel(
    x_ref, out_ref, log_ref,
    x_buf, yf, o_buf, g_buf, xb, lhs, s_buf, sq_buf, spec, acc, fb, rb,
    x_sem, ss_z, rs_z, ss_o, rs_o, ss_far, rs_far, ok_sem, ss_a, rs_a, ss_x, rs_x, ss_f, rs_f,
):
    b, o = lax.axis_index("blk"), lax.axis_index("off")
    x, y, z_lo = b % 4, b // 4 % 4, b // 16
    z_hi, c = o // 2, o % 2
    z = z_hi * 8 + z_lo

    load = pltpu.make_async_copy(x_ref, x_buf, x_sem)
    load.start()

    def device(dx, dy, dz, core):
        zz = (z + dz) % 16
        return (zz % 8 * 16 + (y + dy) % 4 * 4 + (x + dx) % 4, zz // 8 * 2 + core)

    def remote(src, dst, send, recv, to):
        return pltpu.make_async_remote_copy(
            src_ref=src, dst_ref=dst, send_sem=send, recv_sem=recv,
            device_id=to, device_id_type=MESH,
        )

    partner = device(0, 0, 0, 1 - c)
    opposite = device(0, 0, 8, c)
    barrier = pltpu.get_barrier_semaphore()
    peers = [partner] + [device(0, 0, d, c) for d in (-2, -1, 1, 2)]
    for d in (1, 3, 2):
        for core in (0, 1):
            peers += [device(d, 0, 0, core), device(0, d, 0, core)]

    def announce(peer):
        pl.semaphore_signal(barrier, inc=1, device_id=peer, device_id_type=MESH)

    @pl.when(z_hi == 0)
    def _():
        announce(opposite)

    for peer in peers:
        announce(peer)

    place = iota((128, 128), 1)
    source = place // 8 % 2 * 64 + place // 16 * 8 + place % 8
    permute = jnp.where(iota((128, 128), 0) == source, 1.0, 0.0).astype(bf16)
    load.wait()
    yf[...] = nn(x_buf[...].astype(f32).reshape(128, 128).astype(bf16), permute)
    rows = [yf[pl.ds(r, 16, stride=8), :] for r in range(8)]
    for bit in (1, 2, 4):
        upper = lane_bit((16, 128), 16 * bit)
        for r in range(8):
            if r & bit == 0:
                low, high = rows[r], rows[r | bit]
                rows[r] = jnp.where(upper, lane_roll(high, 16 * bit), low)
                rows[r | bit] = jnp.where(upper, high, lane_roll(low, -16 * bit))
    for k in range(8):
        tile = rows[k].astype(bf16)
        g_buf[0, 0, 0, k] = tile
        o_buf[0, c, k] = tile

    pl.semaphore_wait(barrier, len(peers) + z_hi)

    own = g_buf.at[0, 0, 0]
    far_own = g_buf.at[1, 0, 0]

    far_copy = remote(own, far_own, ss_far, rs_far, opposite)

    @pl.when(z_hi == 1)
    def _():
        far_copy.start()
        pl.semaphore_signal(ok_sem, inc=1, device_id=opposite, device_id_type=MESH)

    def z_copy(h, plane):
        return remote(
            g_buf.at[h, 0, 0], g_buf.at[h, plane, 0], ss_z.at[h, plane], rs_z.at[h, plane], device(0, 0, -plane, c)
        )

    def o_copy(h, path):
        return remote(g_buf.at[h, 0, 0], o_buf.at[h, path], ss_o.at[h], rs_o.at[h], partner)

    def half_of(h, plane):
        return (h + (z_lo + plane) // 8) % 2

    def a_copy(h, plane, j):
        return remote(
            g_buf.at[h, plane, 0], g_buf.at[h, plane, j],
            ss_a.at[h, plane, j - 1], rs_a.at[h, plane, j - 1], device(-j * (1 - c), -j * c, 0, c),
        )

    def send_along(h, plane):
        for j in (2, 1, 3):
            a_copy(h, plane, j).start()

    def plane_of(j, d):
        first = (4 * ((y + d) % 4) + x) - (4 * y + (x + j) % 4)
        second = (4 * y + (x + d) % 4) - (4 * ((y + j) % 4) + x)
        return (first * (1 - c) + second * c + 15) // 16 * 2

    def slot(j, d):
        return slot_of[j, -d % 4] * (1 - c) + slot_of[-d % 4, j] * c

    def x_copy(h, plane, j, d, core):
        n = slot(j, d)
        lot = 2 if d == 0 else d // 3
        return remote(
            g_buf.at[h, plane, j], xb.at[half_of(h, plane), c, n],
            ss_x.at[h, core, lot], rs_x.at[h, n // 8], device(d * c, d * (1 - c), 0, core),
        )

    def keep_copy(h, plane, j):
        n = slot(j, 0)
        return pltpu.make_async_copy(
            g_buf.at[h, plane, j], xb.at[half_of(h, plane), c, n], rs_x.at[h, n // 8]
        )

    def send_across(h, plane, j):
        core = 0 if plane == 1 else 1

        def when(d, *more):
            wanted = [] if plane == 1 else [plane_of(j, d) == plane]
            tests = wanted + list(more)
            if not tests:
                return lambda f: f()
            return pl.when(functools.reduce(jnp.logical_and, tests))

        for d in (2, 1, 3):
            when(d)(lambda d=d: x_copy(h, plane, j, d, core).start())
        when(0, c != core)(lambda: x_copy(h, plane, j, 0, core).start())
        when(0, c == core)(lambda: keep_copy(h, plane, j).start())

    def relay(h, plane, j):
        a_copy(h, plane, j).wait_recv()
        send_across(h, plane, j)

    def wait_slots(h, group):
        region = xb.at[0, :, pl.ds(group * 8, 8)]
        pltpu.make_async_copy(region, region, rs_x.at[h, group]).wait()

    def spread(h):
        z_copy(h, 2).start()
        z_copy(h, 1).start()
        o_copy(h, c).start()
        send_along(h, 0)
        send_across(h, 0, 0)

    spread(0)

    def frequency_of(q):
        k, u = q // 16, q % 8
        return 8 * k + (k - u + 8) % 8, q // 8 % 2

    def table(q_dim):
        q, s = iota((128, 128), q_dim), iota((128, 128), 1 - q_dim)
        m, part = frequency_of(q)
        phase = (m * s % 128).astype(f32) * (2.0 * math.pi / 128)
        return jnp.where(part == 0, jnp.cos(phase), -jnp.sin(phase))

    f_high, f_low = split(table(1))
    forward = jnp.concatenate([f_high, f_high, f_low], axis=1)
    b_high, b_low = split(table(0))
    backward = jnp.concatenate([b_high, b_high, b_low], axis=1)

    def matches(k):
        u, t = iota((8, 128), 0), iota((8, 128), 1) % 8
        return (u + t) % 8 == k

    def build_lhs(h):
        squares = jnp.zeros((8, 128), f32)
        for path in (0, 1):
            for k in range(8):
                both = o_buf[h, path, k].astype(f32)
                rows = jnp.where(z_hi == 0, both[:8], both[8:])
                squares = squares + rows * rows
                turned = rotate_parts(rows, 1.0)
                pair = [jnp.where(matches(k)[None], v[:, None, :], 0.0) for v in (rows, turned)]
                block = jnp.concatenate(pair, axis=1).reshape(128, 128)
                lhs[h, k, :, path * 128 : path * 128 + 128] = block.astype(bf16)
        return squares

    def tile_of(h, path, k, group):
        return xb[h, path, group * 8 : group * 8 + 8, k].reshape(128, 128)

    def cross(halves, group, first):
        squares = jnp.zeros((128, 128), f32) if first else sq_buf[group]
        for k in range(8):
            tiles = [tile_of(h, path, k, group) for h in halves for path in (0, 1)]
            for t in tiles:
                wide = t.astype(f32)
                squares = squares + wide * wide
            left = jnp.concatenate([lhs[h, k] for h in halves], axis=1)
            part = nt(left, jnp.concatenate(tiles, axis=1))
            s_buf[group, k] = part if first else s_buf[group, k] + part
        sq_buf[group] = squares

    def pieces(a):
        high, low = split(a)
        rest = (a - high.astype(f32) - low.astype(f32)).astype(bf16)
        return [high, low, rest]

    def forward_planes(h):
        z_copy(h, 1).wait_recv()
        send_along(h, 1)
        send_across(h, 1, 0)
        z_copy(h, 2).wait_recv()
        send_along(h, 2)
        send_across(h, 2, 0)
        for plane in (0, 1, 2):
            for j in (1, 3, 2):
                relay(h, plane, j)

    forward_planes(0)

    @pl.when(z_hi == 0)
    def _():
        pl.semaphore_wait(ok_sem, 1)
        far_copy.start()

    o_copy(0, 1 - c).wait_recv()
    own_squares = build_lhs(0)
    far_copy.wait_recv()
    spread(1)
    for k in range(8):
        o_buf[1, c, k] = g_buf[1, 0, 0, k]
    forward_planes(1)
    o_copy(1, 1 - c).wait_recv()
    own_squares = own_squares + build_lhs(1)
    own_gain = concentration * lax.rsqrt(jnp.sum(own_squares, axis=1, keepdims=True) + epsilon)

    early = z_lo < 6
    for group in (0, 1):
        wait_slots(0, group)

    @pl.when(early)
    def _():
        for group in (0, 1):
            cross((0,), group, True)

    ones = jnp.ones((8, 384), bf16)
    lane = iota((128, 256), 1)
    own_lane = z_hi * 8 - 1000 * (1 - c)

    def filter_group(group):
        norm_squares = nt(ones, jnp.concatenate(pieces(sq_buf[group]), axis=1))
        gain = lax.rsqrt(norm_squares + epsilon) * own_gain
        for i in (0, 2, 4, 6):
            two = [
                jnp.concatenate([s_buf[group, k, ii * 16 : ii * 16 + 16, :] for k in range(8)], axis=0)
                for ii in (i, i + 1)
            ]
            high, low = split(jnp.concatenate(two, axis=1))
            correlation = nn(forward, jnp.concatenate([high, low, high], axis=0))
            scale = jnp.concatenate([gain[i : i + 1], gain[i + 1 : i + 2]], axis=1)
            weights = jnp.exp(correlation * scale)
            if group == 0:
                same = lane - jnp.where(lane >= 128, 129, 0) == own_lane + i
                weights = jnp.where(same, 0.0, weights)
            high, low = split(weights)
            spectral = nn(backward, jnp.concatenate([high, low, high], axis=0))
            rounded = spectral.astype(bf16)
            for ii in (0, 1):
                part = spectral[:, ii * 128 : ii * 128 + 128]
                degree = jnp.broadcast_to(jnp.sum(part[0:1], axis=1, keepdims=True), (8, 128))
                fb[i + ii, 4] = degree if group == 0 else fb[i + ii, 4] + degree
                for k in range(8):
                    spec[k, (i + ii) * 16 : (i + ii) * 16 + 16, :] = rounded[
                        k * 16 : k * 16 + 16, ii * 128 : ii * 128 + 128
                    ]
        for k in range(8):
            keep = jnp.concatenate([matches(k)] * 16, axis=0)
            for h in (0, 1):
                for path in (0, 1):
                    part = nn(spec[k], tile_of(h, path, k, group))
                    n = 2 * h + path
                    if group == 0:
                        acc[n] = part if k == 0 else jnp.where(keep, part, acc[n])
                    else:
                        acc[n] = acc[n] + jnp.where(keep, part, 0.0)

    for group in (0, 1):
        wait_slots(1, group)

        @pl.when(early)
        def _():
            cross((1,), group, False)

        @pl.when(jnp.logical_not(early))
        def _():
            cross((0, 1), group, True)

        filter_group(group)

    for n in range(4):
        pair = acc[n].reshape(8, 16, 128)
        total = pair[:, :8] + rotate_parts(pair[:, 8:], -1.0)
        for i in range(8):
            fb[i, n] = total[i]

    last = remote(fb.at[pl.ds((1 - c) * 4, 4)], rb, ss_f, rs_f, partner)
    last.start()
    last.wait()
    total = fb[pl.ds(c * 4, 4)] + rb[...]
    degree = total[:, 4:5]
    v = (total[:, :4] / degree).reshape(16, 8, 128)
    for bit in (1, 2, 4):
        v = jnp.where(lane_bit(v.shape, bit), pltpu.roll(v, bit, 1), v)
    for bit in (1, 2, 4):
        group = lane_bit(v.shape, 16 * bit)
        row = iota(v.shape, 1) // bit % 2 == 1
        down = lane_roll(pltpu.roll(v, 8 - bit, 1), 16 * bit)
        up = lane_roll(pltpu.roll(v, bit, 1), -16 * bit)
        v = jnp.where(group == row, v, jnp.where(group, down, up))
    flat = sum(nt(p, permute) for p in pieces(v.reshape(128, 128)))
    flat = flat.reshape(4, 4, 8, 128)
    for h in (0, 1):
        for path in (0, 1):
            start = pl.multiple_of(((z_hi + h) % 2 * 2 + path) * 8, 8)
            out_ref[:, pl.ds(start, 8), :] = flat[:, 2 * h + path]
    logs = jnp.log(degree[:, 0])
    pick = iota((8, 128), 1)
    line = jnp.zeros((8, 128), f32)
    for i in range(4):
        line = jnp.where(pick == i, logs[i], line)
    log_ref[...] = line

    far_copy.wait_send()
    for h in (0, 1):
        z_copy(h, 1).wait_send()
        z_copy(h, 2).wait_send()
        o_copy(h, c).wait_send()
        for plane in (0, 1, 2):
            for j in (1, 2, 3):
                a_copy(h, plane, j).wait_send()
        for core in (0, 1):
            for lot, count in enumerate((8, 4)):
                sent = xb.at[0, 0, pl.ds(0, count)]
                remote(sent, sent, ss_x.at[h, core, lot], rs_x.at[h, 0], partner).wait_send()

        def sent_over(core):
            sent = xb.at[0, 0, pl.ds(0, 4)]
            remote(sent, sent, ss_x.at[h, core, 2], rs_x.at[h, 0], partner).wait_send()

        pl.when(c == 0)(functools.partial(sent_over, 1))
        pl.when(c == 1)(functools.partial(sent_over, 0))


def body(coefficients):
    vmem = pl.BlockSpec(memory_space=pltpu.VMEM)
    dma = pltpu.SemaphoreType.DMA
    smoothed, logs = pl.pallas_call(
        body_kernel,
        out_shape=(
            jax.ShapeDtypeStruct((4, 32, 128), f32),
            jax.ShapeDtypeStruct((8, 128), f32),
        ),
        in_specs=[pl.BlockSpec(memory_space=pl.ANY)],
        out_specs=(vmem, vmem),
        scratch_shapes=[
            pltpu.VMEM((16, 8, 128), bf16),
            pltpu.VMEM((128, 128), f32),
            pltpu.VMEM((2, 2, 8, 16, 128), bf16),
            pltpu.VMEM((2, 3, 4, 8, 16, 128), bf16),
            pltpu.VMEM((2, 2, 16, 8, 16, 128), bf16),
            pltpu.VMEM((2, 8, 128, 256), bf16),
            pltpu.VMEM((2, 8, 128, 128), f32),
            pltpu.VMEM((2, 128, 128), f32),
            pltpu.VMEM((8, 128, 128), bf16),
            pltpu.VMEM((4, 128, 128), f32),
            pltpu.VMEM((8, 5, 8, 128), f32),
            pltpu.VMEM((4, 5, 8, 128), f32),
            dma,
            dma((2, 3)), dma((2, 3)),
            dma((2,)), dma((2,)),
            dma, dma,
            pltpu.SemaphoreType.REGULAR,
            dma((2, 3, 3)), dma((2, 3, 3)),
            dma((2, 2, 3)), dma((2, 2)),
            dma, dma,
        ],
        compiler_params=pltpu.CompilerParams(collective_id=0, has_side_effects=True),
        name="graph_filter",
    )(coefficients)
    return smoothed, logs[0, :4]


def solution(mesh):
    return jax.shard_map(
        body,
        mesh=mesh,
        in_specs=(P("blk", "off", None),),
        out_specs=(P(("blk", "off"), None, None), P(("blk", "off"))),
        check_vma=False,
    )
```

time: 52.6 us -> 46.8 us (0.89)
  the two profiles are of different devices: /device:TPU:25 before, /device:TPU:479 now
where the time goes in v2:
time: 46.8 us; the launch traced here: 46.5 us
  Pallas kernels  43.2 us (92%)
  local copies, waits for them, and re-layouts  2.66 us (6%)
  between operations  0.64 us (1%)
    pallas_call x1, Pallas kernels, body(): pl.pallas_call(body_kernel, out_shape=(jax.ShapeDtypeStruct((4, 32, 128),...  43.2 us
    unnamed x1, local copies, waits for them, and re-layouts  1.47 us
    squeeze x1, local copies, waits for them, and re-layouts, body(): return (smoothed, logs[0, :4])  1.19 us

profile of v2, /device:TPU:479, one launch (start us, length us, event | category | flops | bytes accessed | tf_op | source)
XLA Modules:
  0.0 46.5 jit_solution(5175153422441626895)
XLA Ops:
  0.6 43.2 %graph_filter.1 = (f32[4,32,128]{2,1,0:T(8,128)}, f32[8,128]{1,0:T(8,128)}) custom-call(bf16[16,8,128]{2,1,0:T(8,128)(2,1)} %x_ref.1), custom_call_target="tpu_custom_call" | custom-call | tf_op jit(solution)/shard_map/graph_filter/pallas_call | solution.py:402
  43.9 1.2 %slice_bitcast_fusion = f32[4]{0:T(128)} fusion(f32[8,128]{1,0:T(8,128)} %get-tuple-element.5), kind=kLoop, calls=%fused_computation | loop fusion | bytes 32 | tf_op jit(solution)/shard_map/squeeze | solution.py:435
  45.0 1.5 %copy.4 = f32[4,32,128]{2,1,0:T(8,128)} copy(f32[4,32,128]{2,1,0:T(8,128)} %get-tuple-element.8) | data formatting | bytes 131072

commit v3 on v2

--- a/solution.py
+++ b/solution.py
@@ -40,6 +40,17 @@
     return pltpu.roll(a, by % 128, a.ndim - 1)
 
 
+def permutation():
+    place = iota((128, 128), 1)
+    source = place // 8 % 2 * 64 + place // 16 * 8 + place % 8
+    return jnp.where(iota((128, 128), 0) == source, 1.0, 0.0).astype(bf16)
+
+
+def pieces(a):
+    high, low = split(a)
+    return [high, low, (a - high.astype(f32) - low.astype(f32)).astype(bf16)]
+
+
 def rotate_parts(a, sign):
     imag = lane_bit(a.shape, 8)
     return jnp.where(imag, -sign * lane_roll(a, 8), sign * lane_roll(a, -8))
@@ -53,9 +64,9 @@
 
 
 def body_kernel(
-    x_ref, out_ref, log_ref,
+    x_ref, out_ref,
     x_buf, yf, o_buf, g_buf, xb, lhs, s_buf, sq_buf, spec, acc, fb, rb,
-    x_sem, ss_z, rs_z, ss_o, rs_o, ss_far, rs_far, ok_sem, ss_a, rs_a, ss_x, rs_x, ss_f, rs_f,
+    x_sem, ss_z, rs_z, ss_o, rs_o, ss_far, rs_far, ok_sem, wrap_sem, ss_a, rs_a, ss_x, rs_x, ss_f, rs_f,
 ):
     b, o = lax.axis_index("blk"), lax.axis_index("off")
     x, y, z_lo = b % 4, b // 4 % 4, b // 16
@@ -78,7 +89,7 @@
     partner = device(0, 0, 0, 1 - c)
     opposite = device(0, 0, 8, c)
     barrier = pltpu.get_barrier_semaphore()
-    peers = [partner] + [device(0, 0, d, c) for d in (-2, -1, 1, 2)]
+    peers = [partner]
     for d in (1, 3, 2):
         for core in (0, 1):
             peers += [device(d, 0, 0, core), device(0, d, 0, core)]
@@ -93,9 +104,14 @@
     for peer in peers:
         announce(peer)
 
-    place = iota((128, 128), 1)
-    source = place // 8 % 2 * 64 + place // 16 * 8 + place % 8
-    permute = jnp.where(iota((128, 128), 0) == source, 1.0, 0.0).astype(bf16)
+    late = (z + 2) // 16 + (z + 1) // 16
+    first = (z + 15) // 16 + (z + 14) // 16
+    for d in (1, 2):
+        crossing = (z + d) // 16 == 1
+        pl.when(jnp.logical_not(crossing))(lambda d=d: announce(device(0, 0, d, c)))
+        pl.when(z - d < 0)(lambda d=d: announce(device(0, 0, -d, c)))
+
+    permute = permutation()
     load.wait()
     yf[...] = nn(x_buf[...].astype(f32).reshape(128, 128).astype(bf16), permute)
     rows = [yf[pl.ds(r, 16, stride=8), :] for r in range(8)]
@@ -111,21 +127,34 @@
         g_buf[0, 0, 0, k] = tile
         o_buf[0, c, k] = tile
 
-    pl.semaphore_wait(barrier, len(peers) + z_hi)
+    pl.semaphore_wait(barrier, len(peers) + z_hi + late + first)
+    for d in (1, 2):
+        @pl.when((z + d) // 16 == 1)
+        def _():
+            pl.semaphore_signal(
+                wrap_sem, inc=1, device_id=device(0, 0, d, c), device_id_type=MESH
+            )
 
     own = g_buf.at[0, 0, 0]
     far_own = g_buf.at[1, 0, 0]
 
-    far_copy = remote(own, far_own, ss_far, rs_far, opposite)
+    def cut(ref, part):
+        return ref if part is None else ref.at[pl.ds(4 * part, 4)]
+
+    def far_copy(part):
+        return remote(cut(own, part), cut(far_own, part), ss_far.at[part], rs_far.at[part], opposite)
 
     @pl.when(z_hi == 1)
     def _():
-        far_copy.start()
+        far_copy(0).start()
+        far_copy(1).start()
         pl.semaphore_signal(ok_sem, inc=1, device_id=opposite, device_id_type=MESH)
 
-    def z_copy(h, plane):
+    def z_copy(h, plane, part=None):
+        n = part or 0
         return remote(
-            g_buf.at[h, 0, 0], g_buf.at[h, plane, 0], ss_z.at[h, plane], rs_z.at[h, plane], device(0, 0, -plane, c)
+            cut(g_buf.at[h, 0, 0], part), cut(g_buf.at[h, plane, 0], part),
+            ss_z.at[h, plane, n], rs_z.at[h, plane, n], device(0, 0, -plane, c),
         )
 
     def o_copy(h, path):
@@ -134,15 +163,16 @@
     def half_of(h, plane):
         return (h + (z_lo + plane) // 8) % 2
 
-    def a_copy(h, plane, j):
+    def a_copy(h, plane, j, part):
+        n = part or 0
         return remote(
-            g_buf.at[h, plane, 0], g_buf.at[h, plane, j],
-            ss_a.at[h, plane, j - 1], rs_a.at[h, plane, j - 1], device(-j * (1 - c), -j * c, 0, c),
+            cut(g_buf.at[h, plane, 0], part), cut(g_buf.at[h, plane, j], part),
+            ss_a.at[h, plane, j - 1, n], rs_a.at[h, plane, j - 1, n], device(-j * (1 - c), -j * c, 0, c),
         )
 
-    def send_along(h, plane):
+    def send_along(h, plane, part):
         for j in (2, 1, 3):
-            a_copy(h, plane, j).start()
+            a_copy(h, plane, j, part).start()
 
     def plane_of(j, d):
         first = (4 * ((y + d) % 4) + x) - (4 * y + (x + j) % 4)
@@ -152,21 +182,21 @@
     def slot(j, d):
         return slot_of[j, -d % 4] * (1 - c) + slot_of[-d % 4, j] * c
 
-    def x_copy(h, plane, j, d, core):
+    def x_copy(h, plane, j, d, core, part):
         n = slot(j, d)
         lot = 2 if d == 0 else d // 3
         return remote(
-            g_buf.at[h, plane, j], xb.at[half_of(h, plane), c, n],
+            cut(g_buf.at[h, plane, j], part), cut(xb.at[half_of(h, plane), c, n], part),
             ss_x.at[h, core, lot], rs_x.at[h, n // 8], device(d * c, d * (1 - c), 0, core),
         )
 
-    def keep_copy(h, plane, j):
+    def keep_copy(h, plane, j, part):
         n = slot(j, 0)
         return pltpu.make_async_copy(
-            g_buf.at[h, plane, j], xb.at[half_of(h, plane), c, n], rs_x.at[h, n // 8]
+            cut(g_buf.at[h, plane, j], part), cut(xb.at[half_of(h, plane), c, n], part), rs_x.at[h, n // 8]
         )
 
-    def send_across(h, plane, j):
+    def send_across(h, plane, j, part):
         core = 0 if plane == 1 else 1
 
         def when(d, *more):
@@ -177,26 +207,43 @@
             return pl.when(functools.reduce(jnp.logical_and, tests))
 
         for d in (2, 1, 3):
-            when(d)(lambda d=d: x_copy(h, plane, j, d, core).start())
-        when(0, c != core)(lambda: x_copy(h, plane, j, 0, core).start())
-        when(0, c == core)(lambda: keep_copy(h, plane, j).start())
-
-    def relay(h, plane, j):
-        a_copy(h, plane, j).wait_recv()
-        send_across(h, plane, j)
+            when(d)(lambda d=d: x_copy(h, plane, j, d, core, part).start())
+        when(0, c != core)(lambda: x_copy(h, plane, j, 0, core, part).start())
+        when(0, c == core)(lambda: keep_copy(h, plane, j, part).start())
 
     def wait_slots(h, group):
         region = xb.at[0, :, pl.ds(group * 8, 8)]
         pltpu.make_async_copy(region, region, rs_x.at[h, group]).wait()
 
-    def spread(h):
-        z_copy(h, 2).start()
-        z_copy(h, 1).start()
-        o_copy(h, c).start()
-        send_along(h, 0)
-        send_across(h, 0, 0)
-
-    spread(0)
+    def answer_far():
+        @pl.when(z_hi == 0)
+        def _():
+            pl.semaphore_wait(ok_sem, 1)
+            far_copy(0).start()
+            far_copy(1).start()
+
+    def spread(h, part):
+        if h == 0:
+            pl.when(z >= 2)(lambda: z_copy(0, 2).start())
+            pl.when(z >= 1)(lambda: z_copy(0, 1).start())
+        else:
+            z_copy(h, 2, part).start()
+            z_copy(h, 1, part).start()
+        send_along(h, 0, part)
+        send_across(h, 0, 0, part)
+
+    def pass_on(h, plane, part):
+        z_copy(h, plane, part).wait_recv()
+        send_along(h, plane, part)
+        send_across(h, plane, 0, part)
+
+    def relay(h, plane, part):
+        for j in (1, 3, 2):
+            a_copy(h, plane, j, part).wait_recv()
+            send_across(h, plane, j, part)
+
+    o_copy(0, c).start()
+    spread(0, None)
 
     def frequency_of(q):
         k, u = q // 16, q % 8
@@ -223,6 +270,7 @@
             for k in range(8):
                 both = o_buf[h, path, k].astype(f32)
                 rows = jnp.where(z_hi == 0, both[:8], both[8:])
+                rows = jnp.where(c == 0, pltpu.roll(rows, 4, 0), rows)
                 squares = squares + rows * rows
                 turned = rotate_parts(rows, 1.0)
                 pair = [jnp.where(matches(k)[None], v[:, None, :], 0.0) for v in (rows, turned)]
@@ -245,36 +293,36 @@
             s_buf[group, k] = part if first else s_buf[group, k] + part
         sq_buf[group] = squares
 
-    def pieces(a):
-        high, low = split(a)
-        rest = (a - high.astype(f32) - low.astype(f32)).astype(bf16)
-        return [high, low, rest]
-
-    def forward_planes(h):
-        z_copy(h, 1).wait_recv()
-        send_along(h, 1)
-        send_across(h, 1, 0)
-        z_copy(h, 2).wait_recv()
-        send_along(h, 2)
-        send_across(h, 2, 0)
-        for plane in (0, 1, 2):
-            for j in (1, 3, 2):
-                relay(h, plane, j)
-
-    forward_planes(0)
-
-    @pl.when(z_hi == 0)
+    pass_on(0, 1, None)
+    pass_on(0, 2, None)
+    pl.when(z >= 2)(answer_far)
+    for plane in (0, 1, 2):
+        relay(0, plane, None)
+
+    @pl.when(z < 2)
     def _():
-        pl.semaphore_wait(ok_sem, 1)
-        far_copy.start()
+        pl.semaphore_wait(wrap_sem, 2 - z)
+        z_copy(0, 2).start()
+        pl.when(z == 0)(lambda: z_copy(0, 1).start())
+        answer_far()
 
     o_copy(0, 1 - c).wait_recv()
     own_squares = build_lhs(0)
-    far_copy.wait_recv()
-    spread(1)
+    for part in (0, 1):
+        far_copy(part).wait_recv()
+        spread(1, part)
+    o_copy(1, c).start()
     for k in range(8):
         o_buf[1, c, k] = g_buf[1, 0, 0, k]
-    forward_planes(1)
+    for part in (0, 1):
+        pass_on(1, 1, part)
+        pass_on(1, 2, part)
+        if part == 0:
+            relay(1, 0, 0)
+    relay(1, 0, 1)
+    for part in (0, 1):
+        for plane in (1, 2):
+            relay(1, plane, part)
     o_copy(1, 1 - c).wait_recv()
     own_squares = own_squares + build_lhs(1)
     own_gain = concentration * lax.rsqrt(jnp.sum(own_squares, axis=1, keepdims=True) + epsilon)
@@ -292,10 +340,16 @@
     lane = iota((128, 256), 1)
     own_lane = z_hi * 8 - 1000 * (1 - c)
 
+    last = remote(fb.at[pl.ds(0, 4)], rb, ss_f, rs_f, partner)
+
     def filter_group(group):
         norm_squares = nt(ones, jnp.concatenate(pieces(sq_buf[group]), axis=1))
         gain = lax.rsqrt(norm_squares + epsilon) * own_gain
-        for i in (0, 2, 4, 6):
+        for side in (0, 1):
+            filter_side(group, gain, side)
+
+    def filter_side(group, gain, side):
+        for i in (4 * side, 4 * side + 2):
             two = [
                 jnp.concatenate([s_buf[group, k, ii * 16 : ii * 16 + 16, :] for k in range(8)], axis=0)
                 for ii in (i, i + 1)
@@ -318,16 +372,26 @@
                     spec[k, (i + ii) * 16 : (i + ii) * 16 + 16, :] = rounded[
                         k * 16 : k * 16 + 16, ii * 128 : ii * 128 + 128
                     ]
+        rows = pl.ds(side * 64, 64)
+        totals = [None] * 4 if group == 0 else [acc[n, rows] for n in range(4)]
         for k in range(8):
-            keep = jnp.concatenate([matches(k)] * 16, axis=0)
-            for h in (0, 1):
-                for path in (0, 1):
-                    part = nn(spec[k], tile_of(h, path, k, group))
-                    n = 2 * h + path
-                    if group == 0:
-                        acc[n] = part if k == 0 else jnp.where(keep, part, acc[n])
-                    else:
-                        acc[n] = acc[n] + jnp.where(keep, part, 0.0)
+            keep = jnp.concatenate([matches(k)] * 8, axis=0)
+            tiles = [tile_of(h, path, k, group) for h in (0, 1) for path in (0, 1)]
+            product = nn(spec[k, rows], jnp.concatenate(tiles, axis=1))
+            for n in range(4):
+                part = product[:, n * 128 : n * 128 + 128]
+                if group == 0:
+                    totals[n] = part if k == 0 else jnp.where(keep, part, totals[n])
+                else:
+                    totals[n] = totals[n] + jnp.where(keep, part, 0.0)
+        for n in range(4):
+            if group == 0:
+                acc[n, rows] = totals[n]
+            else:
+                pair = totals[n].reshape(4, 16, 128)
+                fb[4 * side : 4 * side + 4, n] = pair[:, :8] + rotate_parts(pair[:, 8:], -1.0)
+        if group == 1 and side == 0:
+            last.start()
 
     for group in (0, 1):
         wait_slots(1, group)
@@ -342,18 +406,38 @@
 
         filter_group(group)
 
-    for n in range(4):
-        pair = acc[n].reshape(8, 16, 128)
-        total = pair[:, :8] + rotate_parts(pair[:, 8:], -1.0)
-        for i in range(8):
-            fb[i, n] = total[i]
-
-    last = remote(fb.at[pl.ds((1 - c) * 4, 4)], rb, ss_f, rs_f, partner)
-    last.start()
     last.wait()
-    total = fb[pl.ds(c * 4, 4)] + rb[...]
-    degree = total[:, 4:5]
-    v = (total[:, :4] / degree).reshape(16, 8, 128)
+    out_ref[...] = fb[4:8] + rb[...]
+
+    for part in (0, 1):
+        far_copy(part).wait_send()
+    for h in (0, 1):
+        parts = (0, 1) if h else (None,)
+        for part in parts:
+            z_copy(h, 1, part).wait_send()
+            z_copy(h, 2, part).wait_send()
+        o_copy(h, c).wait_send()
+        for plane in (0, 1, 2):
+            for j in (1, 2, 3):
+                for part in parts:
+                    a_copy(h, plane, j, part).wait_send()
+        for core in (0, 1):
+            for lot, count in enumerate((8, 4)):
+                sent = xb.at[0, 0, pl.ds(0, count)]
+                remote(sent, sent, ss_x.at[h, core, lot], rs_x.at[h, 0], partner).wait_send()
+
+        def sent_over(core):
+            sent = xb.at[0, 0, pl.ds(0, 4)]
+            remote(sent, sent, ss_x.at[h, core, 2], rs_x.at[h, 0], partner).wait_send()
+
+        pl.when(c == 0)(functools.partial(sent_over, 1))
+        pl.when(c == 1)(functools.partial(sent_over, 0))
+
+
+def order_kernel(total_ref, out_ref, log_ref):
+    z_hi = lax.axis_index("off") // 2
+    degree = total_ref[:, 4:5]
+    v = (total_ref[:, :4] / degree).reshape(16, 8, 128)
     for bit in (1, 2, 4):
         v = jnp.where(lane_bit(v.shape, bit), pltpu.roll(v, bit, 1), v)
     for bit in (1, 2, 4):
@@ -362,51 +446,25 @@
         down = lane_roll(pltpu.roll(v, 8 - bit, 1), 16 * bit)
         up = lane_roll(pltpu.roll(v, bit, 1), -16 * bit)
         v = jnp.where(group == row, v, jnp.where(group, down, up))
-    flat = sum(nt(p, permute) for p in pieces(v.reshape(128, 128)))
-    flat = flat.reshape(4, 4, 8, 128)
+    permute = permutation()
+    flat = sum(nt(p, permute) for p in pieces(v.reshape(128, 128))).reshape(4, 4, 8, 128)
     for h in (0, 1):
         for path in (0, 1):
             start = pl.multiple_of(((z_hi + h) % 2 * 2 + path) * 8, 8)
             out_ref[:, pl.ds(start, 8), :] = flat[:, 2 * h + path]
-    logs = jnp.log(degree[:, 0])
-    pick = iota((8, 128), 1)
-    line = jnp.zeros((8, 128), f32)
+    logs = jnp.log(degree)
     for i in range(4):
-        line = jnp.where(pick == i, logs[i], line)
-    log_ref[...] = line
-
-    far_copy.wait_send()
-    for h in (0, 1):
-        z_copy(h, 1).wait_send()
-        z_copy(h, 2).wait_send()
-        o_copy(h, c).wait_send()
-        for plane in (0, 1, 2):
-            for j in (1, 2, 3):
-                a_copy(h, plane, j).wait_send()
-        for core in (0, 1):
-            for lot, count in enumerate((8, 4)):
-                sent = xb.at[0, 0, pl.ds(0, count)]
-                remote(sent, sent, ss_x.at[h, core, lot], rs_x.at[h, 0], partner).wait_send()
-
-        def sent_over(core):
-            sent = xb.at[0, 0, pl.ds(0, 4)]
-            remote(sent, sent, ss_x.at[h, core, 2], rs_x.at[h, 0], partner).wait_send()
-
-        pl.when(c == 0)(functools.partial(sent_over, 1))
-        pl.when(c == 1)(functools.partial(sent_over, 0))
+        log_ref[i] = logs[i, 0, 0, 0]
 
 
 def body(coefficients):
     vmem = pl.BlockSpec(memory_space=pltpu.VMEM)
     dma = pltpu.SemaphoreType.DMA
-    smoothed, logs = pl.pallas_call(
+    total = pl.pallas_call(
         body_kernel,
-        out_shape=(
-            jax.ShapeDtypeStruct((4, 32, 128), f32),
-            jax.ShapeDtypeStruct((8, 128), f32),
-        ),
-        in_specs=[pl.BlockSpec(memory_space=pl.ANY)],
-        out_specs=(vmem, vmem),
+        out_shape=jax.ShapeDtypeStruct((4, 5, 8, 128), f32),
+        in_specs=[pl.BlockSpec(memory_space=pltpu.MemorySpace.HBM)],
+        out_specs=vmem,
         scratch_shapes=[
             pltpu.VMEM((16, 8, 128), bf16),
             pltpu.VMEM((128, 128), f32),
@@ -421,18 +479,31 @@
             pltpu.VMEM((8, 5, 8, 128), f32),
             pltpu.VMEM((4, 5, 8, 128), f32),
             dma,
-            dma((2, 3)), dma((2, 3)),
+            dma((2, 3, 2)), dma((2, 3, 2)),
             dma((2,)), dma((2,)),
-            dma, dma,
+            dma((2,)), dma((2,)),
             pltpu.SemaphoreType.REGULAR,
-            dma((2, 3, 3)), dma((2, 3, 3)),
+            pltpu.SemaphoreType.REGULAR,
+            dma((2, 3, 3, 2)), dma((2, 3, 3, 2)),
             dma((2, 2, 3)), dma((2, 2)),
             dma, dma,
         ],
-        compiler_params=pltpu.CompilerParams(collective_id=0, has_side_effects=True),
+        compiler_params=pltpu.CompilerParams(
+            collective_id=0, has_side_effects=True, vmem_limit_bytes=32 << 20
+        ),
         name="graph_filter",
     )(coefficients)
-    return smoothed, logs[0, :4]
+    return pl.pallas_call(
+        order_kernel,
+        out_shape=(
+            jax.ShapeDtypeStruct((4, 32, 128), f32),
+            jax.ShapeDtypeStruct((4,), f32),
+        ),
+        in_specs=[vmem],
+        out_specs=(vmem, pl.BlockSpec(memory_space=pltpu.SMEM)),
+        compiler_params=pltpu.CompilerParams(vmem_limit_bytes=8 << 20),
+        name="order",
+    )(total)
 
 
 def solution(mesh):

time: 46.8 us -> 42.2 us (0.902)
  the two profiles are of different devices: /device:TPU:479 before, /device:TPU:25 now
where the time goes in v3:
time: 42.2 us; the launch traced here: 42 us
  Pallas kernels  40.6 us (96%)
  local copies, waits for them, and re-layouts  0.75 us (2%)
  between operations  0.65 us (2%)
    pallas_call x1, Pallas kernels, body(): pl.pallas_call(body_kernel, out_shape=jax.ShapeDtypeStruct((4, 5, 8, 128)...  39.6 us
    pallas_call x1, Pallas kernels, body(): pl.pallas_call(order_kernel, out_shape=(jax.ShapeDtypeStruct((4, 32, 128)...  1.03 us

profile of v3, /device:TPU:25, one launch (start us, length us, event | category | flops | bytes accessed | tf_op | source)
XLA Modules:
  0.0 42.0 jit_solution(5418184959782264035)
XLA Ops:
  0.6 0.0 copy-start
  0.6 0.7 %copy-done = bf16[16,8,128]{2,1,0:T(8,128)(2,1)S(1)} copy-done((bf16[16,8,128]{2,1,0:T(8,128)(2,1)S(1)}, bf16[16,8,128]{2,1,0:T(8,128)(2,1)}, u32[]{:S(2)}) %copy-start) | copy-done | bytes 32792
  1.4 39.6 %graph_filter.1.total_ref = f32[4,5,8,128]{3,2,1,0:T(8,128)S(1)} custom-call(bf16[16,8,128]{2,1,0:T(8,128)(2,1)S(1)} %copy-done), custom_call_target="tpu_custom_call" | custom-call | tf_op jit(solution)/shard_map/graph_filter/pallas_call | solution.py:463
  41.0 1.0 %order.1 = (f32[4,32,128]{2,1,0:T(8,128)}, f32[4]{0:T(128)}) custom-call(f32[4,5,8,128]{3,2,1,0:T(8,128)S(1)} %graph_filter.1.total_ref), custom_call_target="tpu_custom_call" | custom-call | tf_op jit(solution)/shard_map/order/pallas_call | solution.py:496
Async XLA Ops:
  0.6 0.8 %copy-start = (bf16[16,8,128]{2,1,0:T(8,128)(2,1)S(1)}, bf16[16,8,128]{2,1,0:T(8,128)(2,1)}, u32[]{:S(2)}) copy-start(bf16[16,8,128]{2,1,0:T(8,128)(2,1)} %x_ref.1) | copy-start | bytes 98308

commit v4 on v3

--- a/solution.py
+++ b/solution.py
@@ -66,7 +66,7 @@
 def body_kernel(
     x_ref, out_ref,
     x_buf, yf, o_buf, g_buf, xb, lhs, s_buf, sq_buf, spec, acc, fb, rb,
-    x_sem, ss_z, rs_z, ss_o, rs_o, ss_far, rs_far, ok_sem, wrap_sem, ss_a, rs_a, ss_x, rs_x, ss_f, rs_f,
+    x_sem, ss_z, rs_z, ss_o, rs_o, ss_far, rs_far, ok_sem, wrap_sem, next_sem, ss_a, rs_a, ss_x, rs_x, ss_f, rs_f,
 ):
     b, o = lax.axis_index("blk"), lax.axis_index("off")
     x, y, z_lo = b % 4, b // 4 % 4, b // 16
@@ -90,7 +90,7 @@
     opposite = device(0, 0, 8, c)
     barrier = pltpu.get_barrier_semaphore()
     peers = [partner]
-    for d in (1, 3, 2):
+    for d in (1, 3):
         for core in (0, 1):
             peers += [device(d, 0, 0, core), device(0, d, 0, core)]
 
@@ -150,6 +150,11 @@
         far_copy(1).start()
         pl.semaphore_signal(ok_sem, inc=1, device_id=opposite, device_id_type=MESH)
 
+    for dx, dy in ((-1, 0), (0, -1)):
+        pl.semaphore_signal(
+            next_sem, inc=1, device_id=device(dx, dy, 0, c), device_id_type=MESH
+        )
+
     def z_copy(h, plane, part=None):
         n = part or 0
         return remote(
@@ -171,7 +176,9 @@
         )
 
     def send_along(h, plane, part):
-        for j in (2, 1, 3):
+        for j in (1, 3, 2):
+            if (h, plane, j) == (0, 0, 2):
+                pl.semaphore_wait(next_sem, 2)
             a_copy(h, plane, j, part).start()
 
     def plane_of(j, d):
@@ -224,11 +231,11 @@
 
     def spread(h, part):
         if h == 0:
+            pl.when(z >= 1)(lambda: z_copy(0, 1).start())
             pl.when(z >= 2)(lambda: z_copy(0, 2).start())
-            pl.when(z >= 1)(lambda: z_copy(0, 1).start())
         else:
+            z_copy(h, 1, part).start()
             z_copy(h, 2, part).start()
-            z_copy(h, 1, part).start()
         send_along(h, 0, part)
         send_across(h, 0, 0, part)
 
@@ -484,6 +491,7 @@
             dma((2,)), dma((2,)),
             pltpu.SemaphoreType.REGULAR,
             pltpu.SemaphoreType.REGULAR,
+            pltpu.SemaphoreType.REGULAR,
             dma((2, 3, 3, 2)), dma((2, 3, 3, 2)),
             dma((2, 2, 3)), dma((2, 2)),
             dma, dma,

time: 42.2 us -> 40.3 us (0.955)
  Pallas kernels: 40.6 us -> 38.7 us
    pallas_call x1, Pallas kernels: 39.6 us -> 37.7 us  [body(): pl.pallas_call(body_kernel, out_shape=jax.ShapeDtypeStruct((4, 5, 8, 128)...]
where the time goes in v4:
time: 40.3 us; the launch traced here: 40.1 us
  Pallas kernels  38.7 us (96%)
  local copies, waits for them, and re-layouts  0.75 us (2%)
  between operations  0.65 us (2%)
    pallas_call x1, Pallas kernels, body(): pl.pallas_call(body_kernel, out_shape=jax.ShapeDtypeStruct((4, 5, 8, 128)...  37.7 us
    pallas_call x1, Pallas kernels, body(): pl.pallas_call(order_kernel, out_shape=(jax.ShapeDtypeStruct((4, 32, 128)...  1.03 us

profile of v4, /device:TPU:25, one launch (start us, length us, event | category | flops | bytes accessed | tf_op | source)
XLA Modules:
  0.0 40.1 jit_solution(13307672739769613392)
XLA Ops:
  0.6 0.0 copy-start
  0.6 0.7 %copy-done = bf16[16,8,128]{2,1,0:T(8,128)(2,1)S(1)} copy-done((bf16[16,8,128]{2,1,0:T(8,128)(2,1)S(1)}, bf16[16,8,128]{2,1,0:T(8,128)(2,1)}, u32[]{:S(2)}) %copy-start) | copy-done | bytes 32792
  1.4 37.7 %graph_filter.1.total_ref = f32[4,5,8,128]{3,2,1,0:T(8,128)S(1)} custom-call(bf16[16,8,128]{2,1,0:T(8,128)(2,1)S(1)} %copy-done), custom_call_target="tpu_custom_call" | custom-call | tf_op jit(solution)/shard_map/graph_filter/pallas_call | solution.py:470
  39.1 1.0 %order.1 = (f32[4,32,128]{2,1,0:T(8,128)}, f32[4]{0:T(128)}) custom-call(f32[4,5,8,128]{3,2,1,0:T(8,128)S(1)} %graph_filter.1.total_ref), custom_call_target="tpu_custom_call" | custom-call | tf_op jit(solution)/shard_map/order/pallas_call | solution.py:504
Async XLA Ops:
  0.6 0.8 %copy-start = (bf16[16,8,128]{2,1,0:T(8,128)(2,1)S(1)}, bf16[16,8,128]{2,1,0:T(8,128)(2,1)}, u32[]{:S(2)}) copy-start(bf16[16,8,128]{2,1,0:T(8,128)(2,1)} %x_ref.1) | copy-start | bytes 98308

commit v5 on v4

--- a/solution.py
+++ b/solution.py
@@ -65,16 +65,13 @@
 
 def body_kernel(
     x_ref, out_ref,
-    x_buf, yf, o_buf, g_buf, xb, lhs, s_buf, sq_buf, spec, acc, fb, rb,
-    x_sem, ss_z, rs_z, ss_o, rs_o, ss_far, rs_far, ok_sem, wrap_sem, next_sem, ss_a, rs_a, ss_x, rs_x, ss_f, rs_f,
+    yf, o_buf, g_buf, xb, lhs, s_buf, sq_buf, spec, acc, fb, rb,
+    ss_z, rs_z, ss_o, rs_o, ss_far, rs_far, ok_sem, wrap_sem, next_sem, ss_a, rs_a, ss_x, rs_x, ss_f, rs_f,
 ):
     b, o = lax.axis_index("blk"), lax.axis_index("off")
     x, y, z_lo = b % 4, b // 4 % 4, b // 16
     z_hi, c = o // 2, o % 2
     z = z_hi * 8 + z_lo
-
-    load = pltpu.make_async_copy(x_ref, x_buf, x_sem)
-    load.start()
 
     def device(dx, dy, dz, core):
         zz = (z + dz) % 16
@@ -112,8 +109,7 @@
         pl.when(z - d < 0)(lambda d=d: announce(device(0, 0, -d, c)))
 
     permute = permutation()
-    load.wait()
-    yf[...] = nn(x_buf[...].astype(f32).reshape(128, 128).astype(bf16), permute)
+    yf[...] = nn(x_ref[...].astype(f32).reshape(128, 128).astype(bf16), permute)
     rows = [yf[pl.ds(r, 16, stride=8), :] for r in range(8)]
     for bit in (1, 2, 4):
         upper = lane_bit((16, 128), 16 * bit)
@@ -303,7 +299,7 @@
     pass_on(0, 1, None)
     pass_on(0, 2, None)
     pl.when(z >= 2)(answer_far)
-    for plane in (0, 1, 2):
+    for plane in (1, 0, 2):
         relay(0, plane, None)
 
     @pl.when(z < 2)
@@ -321,12 +317,12 @@
     o_copy(1, c).start()
     for k in range(8):
         o_buf[1, c, k] = g_buf[1, 0, 0, k]
-    for part in (0, 1):
-        pass_on(1, 1, part)
-        pass_on(1, 2, part)
-        if part == 0:
-            relay(1, 0, 0)
+    pass_on(1, 1, 0)
+    relay(1, 0, 0)
+    pass_on(1, 2, 0)
+    pass_on(1, 1, 1)
     relay(1, 0, 1)
+    pass_on(1, 2, 1)
     for part in (0, 1):
         for plane in (1, 2):
             relay(1, plane, part)
@@ -470,10 +466,9 @@
     total = pl.pallas_call(
         body_kernel,
         out_shape=jax.ShapeDtypeStruct((4, 5, 8, 128), f32),
-        in_specs=[pl.BlockSpec(memory_space=pltpu.MemorySpace.HBM)],
+        in_specs=[vmem],
         out_specs=vmem,
         scratch_shapes=[
-            pltpu.VMEM((16, 8, 128), bf16),
             pltpu.VMEM((128, 128), f32),
             pltpu.VMEM((2, 2, 8, 16, 128), bf16),
             pltpu.VMEM((2, 3, 4, 8, 16, 128), bf16),
@@ -485,7 +480,6 @@
             pltpu.VMEM((4, 128, 128), f32),
             pltpu.VMEM((8, 5, 8, 128), f32),
             pltpu.VMEM((4, 5, 8, 128), f32),
-            dma,
             dma((2, 3, 2)), dma((2, 3, 2)),
             dma((2,)), dma((2,)),
             dma((2,)), dma((2,)),

time: 40.3 us -> 40.3 us (level)
  no operation moved by 1% of the time
where the time goes in v5:
time: 40.3 us; the launch traced here: 40.1 us
  Pallas kernels  38.7 us (96%)
  local copies, waits for them, and re-layouts  0.75 us (2%)
  between operations  0.65 us (2%)
    pallas_call x1, Pallas kernels, body(): pl.pallas_call(body_kernel, out_shape=jax.ShapeDtypeStruct((4, 5, 8, 128)...  37.7 us
    pallas_call x1, Pallas kernels, body(): pl.pallas_call(order_kernel, out_shape=(jax.ShapeDtypeStruct((4, 32, 128)...  1.03 us

profile of v5, /device:TPU:25, one launch (start us, length us, event | category | flops | bytes accessed | tf_op | source)
XLA Modules:
  0.0 40.1 jit_solution(7732731568792647705)
XLA Ops:
  0.6 0.0 copy-start
  0.6 0.7 %copy-done = bf16[16,8,128]{2,1,0:T(8,128)(2,1)S(1)} copy-done((bf16[16,8,128]{2,1,0:T(8,128)(2,1)S(1)}, bf16[16,8,128]{2,1,0:T(8,128)(2,1)}, u32[]{:S(2)}) %copy-start) | copy-done | bytes 32792
  1.4 37.7 %graph_filter.1.total_ref = f32[4,5,8,128]{3,2,1,0:T(8,128)S(1)} custom-call(bf16[16,8,128]{2,1,0:T(8,128)(2,1)S(1)} %copy-done), custom_call_target="tpu_custom_call" | custom-call | tf_op jit(solution)/shard_map/graph_filter/pallas_call | solution.py:466
  39.1 1.0 %order.1 = (f32[4,32,128]{2,1,0:T(8,128)}, f32[4]{0:T(128)}) custom-call(f32[4,5,8,128]{3,2,1,0:T(8,128)S(1)} %graph_filter.1.total_ref), custom_call_target="tpu_custom_call" | custom-call | tf_op jit(solution)/shard_map/order/pallas_call | solution.py:498
Async XLA Ops:
  0.6 0.8 %copy-start = (bf16[16,8,128]{2,1,0:T(8,128)(2,1)S(1)}, bf16[16,8,128]{2,1,0:T(8,128)(2,1)}, u32[]{:S(2)}) copy-start(bf16[16,8,128]{2,1,0:T(8,128)(2,1)} %x_ref.1) | copy-start | bytes 98308
